TPU v7x, 512 devices: a whole 4x8x8 slice. The times are simulated.
512 devices in a mesh: owner: 128 (over z, y, core), helper: 4 (over x).
Axes of the slice: x: 4, y: 8, z: 8, core: 2. Of those that a mesh axis runs over, the one named last changes fastest.
Arguments:
- embeddings: bfloat16 [196608, 768], P(('owner', 'helper')), may hold values from -16 to 16
- labels: int32 [196608], P(('owner', 'helper')), may hold values from 0 to 32767, as said below
- row_index: int32 [196608], P(('owner', 'helper')), may hold values from 0 to 196607, each once
Outputs:
- nearest: float32 [196608], P(('owner', 'helper'))
Inputs may be any that keep to these rules, and one draw needn't show every extreme that they name: Clusters 64 * k to 64 * k + 63 form cluster group k. The 384 rows of one device carry at most 2 labels of any one group, and in every draw one group receives exactly 2 from every device.
All inputs are finite; a program needn't handle non-finite values.
Results may differ from a plain program's by a relative error of at most 0.00044.
Values may be sent and summed in bfloat16 or wider, within the bound.
No kernel may reach another device: no remote copies, remote signals or barrier semaphores. Data moves between devices by JAX's collectives and lax.ppermute only.
A program may use at most 64 MiB of HBM per device.

v0:
```python
from functools import reduce

import jax
import jax.numpy as jnp
from jax import lax
from jax.sharding import PartitionSpec as P

CLU_DEV = 64


def normalize(embeddings):
    values = embeddings.astype(jnp.float32)
    scale = lax.rsqrt(jnp.mean(values * values, axis=1, keepdims=True) + 1e-06)
    return (values * scale).astype(jnp.bfloat16)


def slot_ranks(target):
    count = target.shape[0]
    order = jnp.arange(count)
    before = order[None, :] < order[:, None]
    same_target = target[:, None] == target[None, :]
    return jnp.sum(same_target & before, axis=1)


def block_length():
    return 512


def masked_max(query_rows, query_label, query_index, key_rows, key_label, key_index):
    scores = (
        jnp.einsum("qd,kd->qk", query_rows, key_rows, preferred_element_type=jnp.float32)
        / query_rows.shape[1]
    )
    keep = (query_label[:, None] == key_label[None, :]) & (
        key_index[None, :] < query_index[:, None]
    )
    return jnp.max(jnp.where(keep, scores, -3.0), axis=1)


def on_device(embeddings, labels, row_index):
    row_count, features = embeddings.shape
    owners = lax.axis_size("owner")
    helpers = lax.axis_size("helper")
    capacity = max(2, 2 * row_count // (owners * helpers))
    unit_rows = normalize(embeddings)
    home_group = labels // CLU_DEV
    places = home_group * capacity + slot_ranks(home_group)
    total = owners * helpers * capacity
    sent_rows = jnp.zeros((total, features), jnp.bfloat16).at[places].set(unit_rows)
    sent_labels = jnp.full((total,), -1, jnp.int32).at[places].set(labels)
    sent_index = jnp.zeros((total,), jnp.int32).at[places].set(row_index)
    step = block_length()
    got_rows, got_labels, got_index = (
        lax.all_to_all(
            lax.all_to_all(
                sent_rows.reshape(owners, helpers, capacity, features),
                "owner",
                split_axis=0,
                concat_axis=0,
                tiled=True,
            ),
            "helper",
            split_axis=1,
            concat_axis=1,
            tiled=True,
        ),
        lax.all_to_all(
            lax.all_to_all(
                sent_labels.reshape(owners, helpers, capacity),
                "owner",
                split_axis=0,
                concat_axis=0,
                tiled=True,
            ),
            "helper",
            split_axis=1,
            concat_axis=1,
            tiled=True,
        ),
        lax.all_to_all(
            lax.all_to_all(
                sent_index.reshape(owners, helpers, capacity),
                "owner",
                split_axis=0,
                concat_axis=0,
                tiled=True,
            ),
            "helper",
            split_axis=1,
            concat_axis=1,
            tiled=True,
        ),
    )
    got_rows = got_rows.reshape(total, features)
    got_labels = got_labels.reshape(total)
    got_index = got_index.reshape(total)
    tiles = [
        (
            got_rows[begin : begin + step],
            got_labels[begin : begin + step],
            got_index[begin : begin + step],
        )
        for begin in range(0, total, step)
    ]
    nearest = jnp.concatenate(
        [
            reduce(jnp.maximum, [masked_max(*query_tile, *key_tile) for key_tile in tiles])
            for query_tile in tiles
        ]
    )
    returned = lax.all_to_all(
        lax.all_to_all(
            nearest.reshape(owners, helpers, capacity),
            "owner",
            split_axis=0,
            concat_axis=0,
            tiled=True,
        ),
        "helper",
        split_axis=1,
        concat_axis=1,
        tiled=True,
    ).reshape(total)
    return jnp.maximum(jnp.take(returned, places), -1.0)


def solution(mesh):
    in_specs = (P(("owner", "helper"), None), P(("owner", "helper")), P(("owner", "helper")))
    out_specs = P(("owner", "helper"))
    return jax.shard_map(
        on_device, mesh=mesh, in_specs=in_specs, out_specs=out_specs, check_vma=False
    )
```

profile of v0, /device:TPU:1, one launch (start us, length us, event | category | flops | bytes accessed | tf_op | source)
XLA Modules:
  0.0 183.0 jit_solution(1470158523616342975)
XLA Ops:
  0.0 0.8 add_select_fusion
  1.0 0.7 compare_select_fusion
  1.7 3.1 %scatter_custom_fusion = s32[1024]{0:T(1024)S(1)} fusion(s32[384]{0:T(512)S(1)} %compare_select_fusion, s32[384]{0:T(512)} %param.4, s32[]{:T(128)} %constant.46.clone.1), kind=kCustom, calls=%fused_computation.38 | custom fusion | bytes 4608 | tf_op jit(solution)/shard_map/scatter | solution.py:50
  5.1 1.5 copy.50
  6.6 18.4 %all-to-all-start = ((s32[128,4,2]{1,2,0:T(2,128)}), s32[128,4,2]{1,2,0:T(2,128)S(1)}, u32[]{:S(2)}, u32[]{:S(2)}) async-start(s32[128,4,2]{1,2,0:T(2,128)} %copy.50), calls=%async_computation | async-start | bytes 262144 | tf_op jit(solution)/shard_map/all_to_all | solution.py:68
  25.0 3.1 %scatter_custom_fusion.1 = s32[1024]{0:T(1024)S(1)} fusion(s32[384]{0:T(512)S(1)} %compare_select_fusion, s32[384]{0:T(512)} %param.5, s32[]{:T(128)} %constant.22.clone.1), kind=kCustom, calls=%fused_computation.36 | custom fusion | bytes 4608 | tf_op jit(solution)/shard_map/scatter | solution.py:51
  28.4 1.5 copy.53
  29.9 7.8 %all-to-all-done = s32[128,4,2]{1,2,0:T(2,128)S(1)} async-done(((s32[128,4,2]{1,2,0:T(2,128)}), s32[128,4,2]{1,2,0:T(2,128)S(1)}, u32[]{:S(2)}, u32[]{:S(2)}) %all-to-all-start) | async-done | bytes 4128 | tf_op jit(solution)/shard_map/all_to_all | solution.py:68
  37.7 5.9 %all-to-all-start.2 = ((s32[128,4,2]{1,2,0:T(2,128)}), s32[128,4,2]{1,2,0:T(2,128)S(1)}, u32[]{:S(2)}, u32[]{:S(2)}) async-start(s32[128,4,2]{1,2,0:T(2,128)} %copy.53), calls=%async_computation.2 | async-start | bytes 262144 | tf_op jit(solution)/shard_map/all_to_all | solution.py:81
  44.5 11.8 %all-to-all-done.2 = s32[128,4,2]{1,2,0:T(2,128)S(1)} async-done(((s32[128,4,2]{1,2,0:T(2,128)}), s32[128,4,2]{1,2,0:T(2,128)S(1)}, u32[]{:S(2)}, u32[]{:S(2)}) %all-to-all-start.2) | async-done | bytes 4128 | tf_op jit(solution)/shard_map/all_to_all | solution.py:81
  56.4 4.0 %all-to-all-start.1 = ((s32[128,4,2]{0,2,1:T(2,128)}), s32[128,4,2]{0,2,1:T(2,128)S(1)}, u32[]{:S(2)}, u32[]{:S(2)}) async-start(s32[128,4,2]{0,2,1:T(2,128)} %copy.51), calls=%async_computation.1 | async-start | bytes 8192 | tf_op jit(solution)/shard_map/all_to_all | solution.py:67
  60.4 2.6 %scatter_custom_fusion.2 = bf16[1024,768]{1,0:T(8,128)(2,1)S(1)} fusion(s32[384]{0:T(512)S(1)} %compare_select_fusion, bf16[]{:T(256)} %constant.50.clone.1, bf16[384,768]{1,0:T(8,128)(2,1)S(1)} %copy-done, f32[384]{0:T(512)S(1)} %add_rsqrt_fusion), kind=kCustom, calls=%fused_computation.20 | custom fusion | flops 884736 | bytes 2164738 | tf_op jit(solution)/shard_map/scatter | solution.py:49
  63.0 1.5 reshape.63
  64.6 7.2 %all-to-all-start.4 = ((bf16[128,4,2,768]{3,2,1,0:T(2,128)(2,1)}), bf16[128,4,2,768]{3,2,1,0:T(2,128)(2,1)S(1)}, u32[]{:S(2)}, u32[]{:S(2)}) async-start(bf16[128,4,2,768]{3,2,1,0:T(2,128)(2,1)} %reshape.63), calls=%async_computation.4 | async-start | bytes 3145728 | tf_op jit(solution)/shard_map/all_to_all | solution.py:55
  71.7 0.7 copy.54
  72.4 40.6 %all-to-all-done.4 = bf16[128,4,2,768]{3,2,1,0:T(2,128)(2,1)S(1)} async-done(((bf16[128,4,2,768]{3,2,1,0:T(2,128)(2,1)}), bf16[128,4,2,768]{3,2,1,0:T(2,128)(2,1)S(1)}, u32[]{:S(2)}, u32[]{:S(2)}) %all-to-all-start.4) | async-done | bytes 1572896 | tf_op jit(solution)/shard_map/all_to_all | solution.py:55
  113.0 3.4 %all-to-all-start.3 = ((s32[128,4,2]{0,2,1:T(2,128)}), s32[128,4,2]{0,2,1:T(2,128)S(1)}, u32[]{:S(2)}, u32[]{:S(2)}) async-start(s32[128,4,2]{0,2,1:T(2,128)} %copy.54), calls=%async_computation.3 | async-start | bytes 8192 | tf_op jit(solution)/shard_map/all_to_all | solution.py:80
  116.5 2.2 %copy.56 = bf16[128,4,2,768]{3,2,0,1:T(2,128)(2,1)} copy(bf16[128,4,2,768]{3,2,1,0:T(2,128)(2,1)S(1)} %all-to-all-done.4) | data formatting | bytes 3145728 | tf_op jit(solution)/shard_map/all_to_all | solution.py:55
  118.7 1.9 %all-to-all-done.3 = s32[128,4,2]{0,2,1:T(2,128)S(1)} async-done(((s32[128,4,2]{0,2,1:T(2,128)}), s32[128,4,2]{0,2,1:T(2,128)S(1)}, u32[]{:S(2)}, u32[]{:S(2)}) %all-to-all-start.3) | async-done | bytes 4128 | tf_op jit(solution)/shard_map/all_to_all | solution.py:80
  120.6 3.6 %all-to-all-start.5 = ((bf16[128,4,2,768]{3,2,0,1:T(2,128)(2,1)}), bf16[128,4,2,768]{3,2,0,1:T(2,128)(2,1)S(1)}, u32[]{:S(2)}, u32[]{:S(2)}) async-start(bf16[128,4,2,768]{3,2,0,1:T(2,128)(2,1)} %copy.56), calls=%async_computation.5 | async-start | bytes 3145728 | tf_op jit(solution)/shard_map/all_to_all | solution.py:54
  125.5 17.4 %all-to-all-done.5 = bf16[128,4,2,768]{3,2,0,1:T(2,128)(2,1)S(1)} async-done(((bf16[128,4,2,768]{3,2,0,1:T(2,128)(2,1)}), bf16[128,4,2,768]{3,2,0,1:T(2,128)(2,1)S(1)}, u32[]{:S(2)}, u32[]{:S(2)}) %all-to-all-start.5) | async-done | bytes 1572896 | tf_op jit(solution)/shard_map/all_to_all | solution.py:54
  142.9 1.1 fusion.21
  145.7 0.7 fusion.7
  146.4 0.7 fusion.6
  147.1 0.7 fusion.5
  147.8 0.7 fusion.4
  149.0 0.9 copy.61
  149.9 22.2 %all_to_all.40 = f32[128,4,2]{1,2,0:T(2,128)S(1)} all-to-all(f32[128,4,2]{1,2,0:T(2,128)S(1)} %copy.61), channel_id=1, replica_groups=mesh['owner'=128,'helper'=4] {'owner'}, dimensions={0} | all-to-all | bytes 8192 | tf_op jit(solution)/shard_map/all_to_all | solution.py:112
  172.1 0.7 copy.62
  172.8 3.2 %all-to-all-start.7 = ((f32[128,4,2]{0,2,1:T(2,128)}), f32[128,4,2]{0,2,1:T(2,128)S(1)}, u32[]{:S(2)}, u32[]{:S(2)}) async-start(f32[128,4,2]{0,2,1:T(2,128)} %copy.62), calls=%async_computation.7 | async-start | bytes 8192 | tf_op jit(solution)/shard_map/all_to_all | solution.py:111
  176.0 4.1 %all-to-all-done.7 = f32[128,4,2]{0,2,1:T(2,128)S(1)} async-done(((f32[128,4,2]{0,2,1:T(2,128)}), f32[128,4,2]{0,2,1:T(2,128)S(1)}, u32[]{:S(2)}, u32[]{:S(2)}) %all-to-all-start.7) | async-done | bytes 4128 | tf_op jit(solution)/shard_map/all_to_all | solution.py:111
  180.6 1.9 %gather_fusion = f32[384]{0:T(512)S(1)} fusion(f32[1024]{0:T(1024)S(1)} %reshape.64, s32[1024]{0:T(1024)S(1)} %pad_clamp_fusion), kind=kCustom, calls=%fused_computation | custom fusion | bytes 4608 | tf_op jit(solution)/shard_map/jit(_take)/gather | solution.py:124
  (32 shorter events, 6.2 us)
Async XLA Ops:
  0.0 43.7 %copy-start = (bf16[384,768]{1,0:T(8,128)(2,1)S(1)}, bf16[384,768]{1,0:T(8,128)(2,1)}, u32[]{:S(2)}) copy-start(bf16[384,768]{1,0:T(8,128)(2,1)} %param.3) | copy-start | bytes 1769476
  6.6 31.1 %all-to-all-start = ((s32[128,4,2]{1,2,0:T(2,128)}), s32[128,4,2]{1,2,0:T(2,128)S(1)}, u32[]{:S(2)}, u32[]{:S(2)}) async-start(s32[128,4,2]{1,2,0:T(2,128)} %copy.50), calls=%async_computation | async-start | bytes 262144 | tf_op jit(solution)/shard_map/all_to_all | solution.py:68
  37.7 18.6 %all-to-all-start.2 = ((s32[128,4,2]{1,2,0:T(2,128)}), s32[128,4,2]{1,2,0:T(2,128)S(1)}, u32[]{:S(2)}, u32[]{:S(2)}) async-start(s32[128,4,2]{1,2,0:T(2,128)} %copy.53), calls=%async_computation.2 | async-start | bytes 262144 | tf_op jit(solution)/shard_map/all_to_all | solution.py:81
  56.4 8.2 %all-to-all-start.1 = ((s32[128,4,2]{0,2,1:T(2,128)}), s32[128,4,2]{0,2,1:T(2,128)S(1)}, u32[]{:S(2)}, u32[]{:S(2)}) async-start(s32[128,4,2]{0,2,1:T(2,128)} %copy.51), calls=%async_computation.1 | async-start | bytes 8192 | tf_op jit(solution)/shard_map/all_to_all | solution.py:67
  64.6 48.5 %all-to-all-start.4 = ((bf16[128,4,2,768]{3,2,1,0:T(2,128)(2,1)}), bf16[128,4,2,768]{3,2,1,0:T(2,128)(2,1)S(1)}, u32[]{:S(2)}, u32[]{:S(2)}) async-start(bf16[128,4,2,768]{3,2,1,0:T(2,128)(2,1)} %reshape.63), calls=%async_computation.4 | async-start | bytes 3145728 | tf_op jit(solution)/shard_map/all_to_all | solution.py:55
  113.0 7.6 %all-to-all-start.3 = ((s32[128,4,2]{0,2,1:T(2,128)}), s32[128,4,2]{0,2,1:T(2,128)S(1)}, u32[]{:S(2)}, u32[]{:S(2)}) async-start(s32[128,4,2]{0,2,1:T(2,128)} %copy.54), calls=%async_computation.3 | async-start | bytes 8192 | tf_op jit(solution)/shard_map/all_to_all | solution.py:80
  120.6 22.3 %all-to-all-start.5 = ((bf16[128,4,2,768]{3,2,0,1:T(2,128)(2,1)}), bf16[128,4,2,768]{3,2,0,1:T(2,128)(2,1)S(1)}, u32[]{:S(2)}, u32[]{:S(2)}) async-start(bf16[128,4,2,768]{3,2,0,1:T(2,128)(2,1)} %copy.56), calls=%async_computation.5 | async-start | bytes 3145728 | tf_op jit(solution)/shard_map/all_to_all | solution.py:54
  172.8 7.4 %all-to-all-start.7 = ((f32[128,4,2]{0,2,1:T(2,128)}), f32[128,4,2]{0,2,1:T(2,128)S(1)}, u32[]{:S(2)}, u32[]{:S(2)}) async-start(f32[128,4,2]{0,2,1:T(2,128)} %copy.62), calls=%async_computation.7 | async-start | bytes 8192 | tf_op jit(solution)/shard_map/all_to_all | solution.py:111
where the time goes:
time: 184 us; the launch traced here: 183 us
  waiting for transfers between devices  83.7 us (45%)
  starting transfers between devices  45.7 us (25%)
  local copies, waits for them, and re-layouts  23.2 us (13%)
  blocking collectives  22.2 us (12%)
  other arithmetic  5.19 us (3%)
  matrix products  2.74 us (1%)
    all_to_all x1, waiting for transfers between devices, on_device(): lax.all_to_all(sent_rows.reshape(owners, helpers, capacity, features), 'o...  40.6 us
    all_to_all x1, blocking collectives, on_device(): lax.all_to_all(nearest.reshape(owners, helpers, capacity), 'owner', split...  22.2 us
    all_to_all x1, starting transfers between devices, on_device(): lax.all_to_all(sent_labels.reshape(owners, helpers, capacity), 'owner', s...  18.4 us
    all_to_all x1, waiting for transfers between devices, on_device(): lax.all_to_all(lax.all_to_all(sent_rows.reshape(owners, helpers, capacity...  17.4 us
    all_to_all x1, waiting for transfers between devices, on_device(): lax.all_to_all(sent_index.reshape(owners, helpers, capacity), 'owner', sp...  11.8 us
    all_to_all x1, waiting for transfers between devices, on_device(): lax.all_to_all(sent_labels.reshape(owners, helpers, capacity), 'owner', s...  7.81 us
    all_to_all x1, starting transfers between devices, on_device(): lax.all_to_all(sent_rows.reshape(owners, helpers, capacity, features), 'o...  7.16 us
    all_to_all x1, starting transfers between devices, on_device(): lax.all_to_all(sent_index.reshape(owners, helpers, capacity), 'owner', sp...  5.92 us
  transfers between devices with their start and end apart: 7, of which 6 were waited for; matrix products, arithmetic and copies ran while one was open for 8% of the time, Pallas kernels for 0%

commit v1 on v0

v1 whole, which is shorter than its diff:
```python
import jax
import jax.numpy as jnp
from jax import lax
from jax.experimental import pallas as pl
from jax.experimental.pallas import tpu as pltpu
from jax.sharding import PartitionSpec as P

CLU_DEV = 64
CAP = 2
LANES = 128
BASE = 64
AXES = ("owner", "helper")


def build_slots(emb_ref, label_ref, index_ref, slots_ref, place_ref):
    rows, features = emb_ref.shape
    values = emb_ref[...].astype(jnp.float32)
    scale = lax.rsqrt(jnp.sum(values * values, axis=1, keepdims=True) / features + 1e-06)
    unit = (values * scale).astype(jnp.bfloat16)

    label = label_ref[...]
    order = index_ref[...]
    group = label // CLU_DEV
    zero = jnp.zeros_like(label)
    table = jnp.concatenate(
        [
            label - group * CLU_DEV,
            order % BASE,
            (order // BASE) % BASE,
            order // (BASE * BASE),
            zero + 1,
            group,
            zero,
            zero,
        ],
        axis=0,
    ).astype(jnp.float32)
    columns = table.T
    group_column = columns[:, 5:6]
    group_row = group.astype(jnp.float32)
    earlier = lax.broadcasted_iota(jnp.int32, (rows, rows), 0) < lax.broadcasted_iota(
        jnp.int32, (rows, rows), 1
    )
    rank = jnp.sum(
        jnp.where((group_column == group_row) & earlier, 1.0, 0.0), axis=0, keepdims=True
    )
    place = group * CAP + rank.astype(jnp.int32)
    place_ref[...] = place

    total = slots_ref.shape[0]
    chosen = jnp.where(
        lax.broadcasted_iota(jnp.int32, (total, rows), 0) == place, 1.0, 0.0
    ).astype(jnp.bfloat16)
    slots_ref[:, :features] = jnp.dot(
        chosen, unit, preferred_element_type=jnp.float32
    ).astype(jnp.bfloat16)
    meta = jnp.concatenate(
        [columns, jnp.zeros((rows, LANES - columns.shape[1]), jnp.float32)], axis=1
    ).astype(jnp.bfloat16)
    slots_ref[:, features:] = jnp.dot(
        chosen, meta, preferred_element_type=jnp.float32
    ).astype(jnp.bfloat16)


def keys_of(label, low, middle, high, filled):
    start = label * float(BASE**3)
    key = start + (high * float(BASE * BASE) + middle * float(BASE) + low)
    return start, jnp.where(filled > 0.5, key, -1.0)


def nearest_earlier(rows_ref, out_ref, wide_ref):
    total = rows_ref.shape[0]
    features = rows_ref.shape[1] - LANES
    keys = rows_ref[:, :features]
    meta = rows_ref[:, features:].astype(jnp.float32)
    flat = meta.T
    _, key_row = keys_of(*(flat[k : k + 1, :] for k in range(5)))
    start_column, key_column = keys_of(*(meta[:, k : k + 1] for k in range(5)))
    step = 256
    for begin in range(0, total, step):
        part = slice(begin, begin + step)
        scores = lax.dot_general(
            rows_ref[part, :features],
            keys,
            (((1,), (1,)), ((), ())),
            preferred_element_type=jnp.float32,
        )
        keep = (key_row >= start_column[part]) & (key_row < key_column[part])
        best = jnp.max(jnp.where(keep, scores, -3.0 * features), axis=1, keepdims=True)
        best = jnp.maximum(best / features, -1.0)
        wide_ref[part, :] = jnp.broadcast_to(best, (step, LANES))
    first = wide_ref[pl.ds(0, total // CAP, stride=CAP), :]
    second = wide_ref[pl.ds(1, total // CAP, stride=CAP), :]
    lane = lax.broadcasted_iota(jnp.int32, first.shape, 1)
    out_ref[...] = jnp.where(lane == 0, first, second)


def pick(returned_ref, place_ref, out_ref):
    count = returned_ref.shape[0]
    rows = place_ref.shape[1]
    place = place_ref[...]
    group = place // CAP
    second = (place - group * CAP) > 0
    value = jnp.where(second, returned_ref[:, 1:2], returned_ref[:, 0:1])
    mine = lax.broadcasted_iota(jnp.int32, (count, rows), 0) == group
    out_ref[...] = jnp.sum(jnp.where(mine, value, 0.0), axis=0, keepdims=True)


def on_device(embeddings, labels, row_index):
    rows, features = embeddings.shape
    devices = lax.axis_size("owner") * lax.axis_size("helper")
    total = devices * CAP
    wide = features + LANES
    slots, place = pl.pallas_call(
        build_slots,
        out_shape=(
            jax.ShapeDtypeStruct((total, wide), jnp.bfloat16),
            jax.ShapeDtypeStruct((1, rows), jnp.int32),
        ),
        name="build_slots",
    )(embeddings, labels.reshape(1, rows), row_index.reshape(1, rows))
    got = lax.all_to_all(
        slots.reshape(devices, CAP, wide), AXES, split_axis=0, concat_axis=0, tiled=True
    )
    nearest = pl.pallas_call(
        nearest_earlier,
        out_shape=jax.ShapeDtypeStruct((devices, LANES), jnp.float32),
        scratch_shapes=[pltpu.VMEM((total, LANES), jnp.float32)],
        name="nearest_earlier",
    )(got.reshape(total, wide))
    returned = lax.all_to_all(
        nearest.reshape(devices, 1, LANES), AXES, split_axis=0, concat_axis=0, tiled=True
    )
    return pl.pallas_call(
        pick,
        out_shape=jax.ShapeDtypeStruct((1, rows), jnp.float32),
        name="pick",
    )(returned.reshape(devices, LANES), place).reshape(rows)


def solution(mesh):
    in_specs = (P(AXES, None), P(AXES), P(AXES))
    return jax.shard_map(
        on_device, mesh=mesh, in_specs=in_specs, out_specs=P(AXES), check_vma=False
    )
```

time: 184 us -> 121 us (0.66)
  waiting for transfers between devices: 83.7 us -> 0 us
  blocking collectives: 22.2 us -> 97.5 us
  starting transfers between devices: 45.7 us -> 0 us
  local copies, waits for them, and re-layouts: 23.2 us -> 11.4 us
  Pallas kernels: 0 us -> 10.1 us
  other arithmetic: 5.19 us -> 1.26 us
  matrix products: 2.74 us -> 0 us
    all_to_all x7 -> x0, waiting for transfers between devices: 83.7 us -> none  [the longest x1 40.6 us: on_device(): lax.all_to_all(sent_rows.reshape(owners, helpers, capacity, features), 'o...]
    all_to_all x1 -> x2, blocking collectives: 22.2 us -> 97.5 us  [the longest x1 70.7 us: on_device(): lax.all_to_all(slots.reshape(devices, CAP, wide), AXES, split_axis=0, con...]
    all_to_all x7 -> x0, starting transfers between devices: 45.7 us -> none  [the longest x1 18.4 us: on_device(): lax.all_to_all(sent_labels.reshape(owners, helpers, capacity), 'owner', s...]
    pallas_call x0 -> x3, Pallas kernels: none -> 10.1 us  [the longest x1 4.43 us: on_device(): pl.pallas_call(nearest_earlier, out_shape=jax.ShapeDtypeStruct((devices,...]
    scatter x2 -> x0, local copies, waits for them, and re-layouts: 6.16 us -> none  [the longest x1 3.08 us: on_device(): sent_index = jnp.zeros((total,), jnp.int32).at[places].set(row_index)]
    reshape x6 -> x4, local copies, waits for them, and re-layouts: 5.4 us -> 11.4 us  [the longest x1 4.98 us: on_device(): got.reshape(total, wide)]
    all_to_all x5 -> x0, local copies, waits for them, and re-layouts: 4.43 us -> none  [the longest x1 2.23 us: on_device(): lax.all_to_all(sent_rows.reshape(owners, helpers, capacity, features), 'o...]
    slice x11 -> x0, local copies, waits for them, and re-layouts: 3.43 us -> none  [the longest x5 2.76 us: on_device(): got_rows[begin:begin + step]]
  transfers between devices with their start and end apart: 7 -> 0, of which waited for: 6 -> 0; matrix products, arithmetic and copies ran while one was open for 8% -> 0% of each run, Pallas kernels for 0% -> 0%
where the time goes in v1:
time: 121 us; the launch traced here: 120 us
  blocking collectives  97.5 us (81%)
  local copies, waits for them, and re-layouts  11.4 us (9%)
  Pallas kernels  10.1 us (8%)
  other arithmetic  1.26 us (1%)
    all_to_all x1, blocking collectives, on_device(): lax.all_to_all(slots.reshape(devices, CAP, wide), AXES, split_axis=0, con...  70.7 us
    all_to_all x1, blocking collectives, on_device(): lax.all_to_all(nearest.reshape(devices, 1, LANES), AXES, split_axis=0, co...  26.8 us
    reshape x1, local copies, waits for them, and re-layouts, on_device(): got.reshape(total, wide)  4.98 us
    pallas_call x1, Pallas kernels, on_device(): pl.pallas_call(nearest_earlier, out_shape=jax.ShapeDtypeStruct((devices,...  4.43 us
    reshape x1, local copies, waits for them, and re-layouts, on_device(): slots.reshape(devices, CAP, wide)  3.91 us
    pallas_call x1, Pallas kernels, on_device(): pl.pallas_call(build_slots, out_shape=(jax.ShapeDtypeStruct((total, wide)...  3.85 us

profile of v1, /device:TPU:1, one launch (start us, length us, event | category | flops | bytes accessed | tf_op | source)
XLA Modules:
  0.0 120.3 jit_solution(7573736117258771116)
XLA Ops:
  0.0 1.2 %reshape.21.label_ref = s32[1,384]{1,0:T(1,128)} reshape(s32[384]{0:T(512)} %param.4) | data formatting | bytes 3072 | tf_op jit(solution)/shard_map/reshape | solution.py:121
  1.2 1.3 %reshape.22.index_ref = s32[1,384]{1,0:T(1,128)} reshape(s32[384]{0:T(512)} %param.5) | data formatting | bytes 3072 | tf_op jit(solution)/shard_map/reshape | solution.py:121
  2.5 3.8 %build_slots.1 = (bf16[1024,896]{1,0:T(8,128)(2,1)}, s32[1,384]{1,0:T(1,128)}) custom-call(bf16[384,768]{1,0:T(8,128)(2,1)} %emb_ref.1, s32[1,384]{1,0:T(1,128)} %reshape.21.label_ref, s32[1,384]{1,0:T(1,128)} %reshape.22.index_ref), custom_call_target="tpu_custom_call" | custom-call | tf_op jit(solution)/shard_map/build_slots/pallas_call | solution.py:114
  6.4 3.9 %reshape.23 = bf16[512,2,896]{2,1,0:T(2,128)(2,1)S(1)} reshape(bf16[1024,896]{1,0:T(8,128)(2,1)} %get-tuple-element.7) | data formatting | bytes 3670016 | tf_op jit(solution)/shard_map/reshape | solution.py:123
  10.3 70.7 %all_to_all.10 = bf16[512,2,896]{2,1,0:T(2,128)(2,1)} all-to-all(bf16[512,2,896]{2,1,0:T(2,128)(2,1)S(1)} %reshape.23), channel_id=1, replica_groups=mesh['owner'=128,'helper'=4] {'owner','helper'}, dimensions={0} | all-to-all | bytes 3670016 | tf_op jit(solution)/shard_map/all_to_all | solution.py:122
  81.0 5.0 %reshape.24.rows_ref = bf16[1024,896]{1,0:T(8,128)(2,1)} reshape(bf16[512,2,896]{2,1,0:T(2,128)(2,1)} %all_to_all.10) | data formatting | bytes 3670016 | tf_op jit(solution)/shard_map/reshape | solution.py:130
  86.0 4.4 %nearest_earlier.1 = f32[512,128]{1,0:T(8,128)} custom-call(bf16[1024,896]{1,0:T(8,128)(2,1)} %reshape.24.rows_ref), custom_call_target="tpu_custom_call" | custom-call | tf_op jit(solution)/shard_map/nearest_earlier/pallas_call | solution.py:125
  90.4 26.8 %all_to_all.11 = f32[512,1,128]{2,1,0:T(1,128)} all-to-all(f32[512,1,128]{2,1,0:T(1,128)} %bitcast.5), channel_id=1, replica_groups=mesh['owner'=128,'helper'=4] {'owner','helper'}, dimensions={0} | all-to-all | bytes 524288 | tf_op jit(solution)/shard_map/all_to_all | solution.py:131
  117.2 1.8 %pick.1 = f32[1,384]{1,0:T(1,128)} custom-call(f32[512,128]{1,0:T(8,128)} %bitcast.4, s32[1,384]{1,0:T(1,128)} %get-tuple-element.8.place_ref), custom_call_target="tpu_custom_call" | custom-call | tf_op jit(solution)/shard_map/pick/pallas_call | solution.py:134
  119.0 1.3 %reduce = f32[384]{0:T(512)} reduce(f32[1,384]{1,0:T(1,128)} %pick.1, f32[]{:T(128)} %constant.3), dimensions={0}, to_apply=%pallas_call.15.reduce_sub_computation | reduce | bytes 3076 | tf_op jit(solution)/shard_map/pick/pallas_call | solution.py:134

commit v2 on v1

v2 whole, which is shorter than its diff:
```python
import jax
import jax.numpy as jnp
from jax import lax
from jax.experimental import pallas as pl
from jax.experimental.pallas import tpu as pltpu
from jax.sharding import PartitionSpec as P

CLU_DEV = 64
CAP = 2
LANES = 128
BASE = 64
AXES = ("owner", "helper")


def build_slots(emb_ref, label_ref, index_ref, slots_ref, place_ref, block_ref, sems):
    rows, features = emb_ref.shape
    blocks, count = block_ref.shape[:2]
    values = emb_ref[...].astype(jnp.float32)
    scale = lax.rsqrt(jnp.sum(values * values, axis=1, keepdims=True) / features + 1e-06)
    unit = (values * scale).astype(jnp.bfloat16)

    label = label_ref[...].reshape(1, rows)
    order = index_ref[...].reshape(1, rows)
    group = label // CLU_DEV
    zero = jnp.zeros_like(label)
    table = jnp.concatenate(
        [
            label - group * CLU_DEV,
            order % BASE,
            (order // BASE) % BASE,
            order // (BASE * BASE),
            zero + 1,
            group,
            zero,
            zero,
        ],
        axis=0,
    ).astype(jnp.float32)
    columns = table.T
    group_column = columns[:, 5:6]
    group_row = group.astype(jnp.float32)
    earlier = lax.broadcasted_iota(jnp.int32, (rows, rows), 0) < lax.broadcasted_iota(
        jnp.int32, (rows, rows), 1
    )
    rank = jnp.sum(
        jnp.where((group_column == group_row) & earlier, 1.0, 0.0), axis=0, keepdims=True
    )
    place = group * CAP + rank.astype(jnp.int32)
    place_ref[...] = place

    total = count * CAP
    chosen = jnp.where(
        lax.broadcasted_iota(jnp.int32, (total, rows), 0) == place, 1.0, 0.0
    ).astype(jnp.bfloat16)
    meta = jnp.concatenate(
        [columns, jnp.zeros((rows, LANES - columns.shape[1]), jnp.float32)], axis=1
    ).astype(jnp.bfloat16)
    copies = []
    for block in range(blocks):
        part = meta if block == blocks - 1 else unit[:, block * LANES : (block + 1) * LANES]
        block_ref[block] = (
            jnp.dot(chosen, part, preferred_element_type=jnp.float32)
            .astype(jnp.bfloat16)
            .reshape(count, CAP, LANES)
        )
        copy = pltpu.make_async_copy(
            block_ref.at[block], slots_ref.at[:, block], sems.at[block]
        )
        copy.start()
        copies.append(copy)
    for copy in copies:
        copy.wait()


def keys_of(label, low, middle, high, filled):
    start = label * float(BASE**3)
    key = start + (high * float(BASE * BASE) + middle * float(BASE) + low)
    return start, jnp.where(filled > 0.5, key, -1.0)


def nearest_earlier(got_ref, out_ref, block_ref, rows_ref, wide_ref, sems):
    blocks, count = block_ref.shape[:2]
    total = count * CAP
    features = (blocks - 1) * LANES
    copies = [
        pltpu.make_async_copy(got_ref.at[:, block], block_ref.at[block], sems.at[block])
        for block in range(blocks)
    ]
    for copy in copies[::-1]:
        copy.start()
    copies[-1].wait()
    meta = block_ref[blocks - 1].reshape(total, LANES).astype(jnp.float32)
    flat = meta.T
    _, key_row = keys_of(*(flat[k : k + 1, :] for k in range(5)))
    start_column, key_column = keys_of(*(meta[:, k : k + 1] for k in range(5)))
    for block in range(blocks - 2, -1, -1):
        copies[block].wait()
        rows_ref[:, block * LANES : (block + 1) * LANES] = block_ref[block].reshape(total, LANES)
    step = 256
    for begin in range(0, total, step):
        part = slice(begin, begin + step)
        scores = lax.dot_general(
            rows_ref[part, :],
            rows_ref[...],
            (((1,), (1,)), ((), ())),
            preferred_element_type=jnp.float32,
        )
        keep = (key_row >= start_column[part]) & (key_row < key_column[part])
        best = jnp.max(jnp.where(keep, scores, -3.0 * features), axis=1, keepdims=True)
        best = jnp.maximum(best / features, -1.0)
        wide_ref[part, :] = jnp.broadcast_to(best, (step, LANES))
    first = wide_ref[pl.ds(0, count, stride=CAP), :]
    second = wide_ref[pl.ds(1, count, stride=CAP), :]
    lane = lax.broadcasted_iota(jnp.int32, first.shape, 1)
    out_ref[...] = jnp.where(lane == 0, first, second)


def pick(returned_ref, place_ref, out_ref):
    count = returned_ref.shape[0]
    rows = place_ref.shape[1]
    place = place_ref[...]
    group = place // CAP
    second = (place - group * CAP) > 0
    value = jnp.where(second, returned_ref[:, 1:2], returned_ref[:, 0:1])
    mine = lax.broadcasted_iota(jnp.int32, (count, rows), 0) == group
    out_ref[...] = jnp.sum(jnp.where(mine, value, 0.0), axis=0)


def on_device(embeddings, labels, row_index):
    rows, features = embeddings.shape
    devices = lax.axis_size("owner") * lax.axis_size("helper")
    total = devices * CAP
    blocks = features // LANES + 1
    anywhere = pl.BlockSpec(memory_space=pl.ANY)
    vmem = pl.BlockSpec(memory_space=pltpu.VMEM)
    slots, place = pl.pallas_call(
        build_slots,
        out_shape=(
            jax.ShapeDtypeStruct((devices, blocks, CAP, LANES), jnp.bfloat16),
            jax.ShapeDtypeStruct((1, rows), jnp.int32),
        ),
        out_specs=(anywhere, vmem),
        scratch_shapes=[
            pltpu.VMEM((blocks, devices, CAP, LANES), jnp.bfloat16),
            pltpu.SemaphoreType.DMA((blocks,)),
        ],
        name="build_slots",
    )(embeddings, labels, row_index)
    got = lax.all_to_all(slots, AXES, split_axis=0, concat_axis=0, tiled=True)
    nearest = pl.pallas_call(
        nearest_earlier,
        out_shape=jax.ShapeDtypeStruct((devices, LANES), jnp.float32),
        in_specs=[anywhere],
        scratch_shapes=[
            pltpu.VMEM((blocks, devices, CAP, LANES), jnp.bfloat16),
            pltpu.VMEM((total, features), jnp.bfloat16),
            pltpu.VMEM((total, LANES), jnp.float32),
            pltpu.SemaphoreType.DMA((blocks,)),
        ],
        name="nearest_earlier",
    )(got)
    returned = lax.all_to_all(
        nearest.reshape(devices, 1, LANES), AXES, split_axis=0, concat_axis=0, tiled=True
    )
    return pl.pallas_call(
        pick, out_shape=jax.ShapeDtypeStruct((rows,), jnp.float32), name="pick"
    )(returned.reshape(devices, LANES), place)


def solution(mesh):
    in_specs = (P(AXES, None), P(AXES), P(AXES))
    return jax.shard_map(
        on_device, mesh=mesh, in_specs=in_specs, out_specs=P(AXES), check_vma=False
    )
```

time: 121 us -> 112 us (0.926)
  local copies, waits for them, and re-layouts: 11.4 us -> 0 us
  Pallas kernels: 10.1 us -> 13.9 us
  other arithmetic: 1.26 us -> 0 us
    reshape x4 -> x0, local copies, waits for them, and re-layouts: 11.4 us -> none  [the longest x1 4.98 us: on_device(): got.reshape(total, wide)]
    pallas_call x1, Pallas kernels: 4.43 us -> 7.44 us  [on_device(): pl.pallas_call(nearest_earlier, out_shape=jax.ShapeDtypeStruct((devices,...]
    pallas_call x1 -> x0, other arithmetic: 1.26 us -> none  [on_device(): pl.pallas_call(pick, out_shape=jax.ShapeDtypeStruct((1, rows), jnp.float3...]
where the time goes in v2:
time: 112 us
  blocking collectives  97.7 us (87%)
  Pallas kernels  13.9 us (12%)
    all_to_all x1, blocking collectives, on_device(): got = lax.all_to_all(slots, AXES, split_axis=0, concat_axis=0, tiled=True)  70.9 us
    all_to_all x1, blocking collectives, on_device(): lax.all_to_all(nearest.reshape(devices, 1, LANES), AXES, split_axis=0, co...  26.8 us
    pallas_call x1, Pallas kernels, on_device(): pl.pallas_call(nearest_earlier, out_shape=jax.ShapeDtypeStruct((devices,...  7.44 us
    pallas_call x1, Pallas kernels, on_device(): pl.pallas_call(build_slots, out_shape=(jax.ShapeDtypeStruct((devices, blo...  4.63 us

profile of v2, /device:TPU:1, one launch (start us, length us, event | category | flops | bytes accessed | tf_op | source)
XLA Modules:
  0.0 111.6 jit_solution(2042477331195639592)
XLA Ops:
  0.0 4.6 %build_slots.1 = (bf16[512,7,2,128]{3,2,1,0:T(2,128)(2,1)}, s32[1,384]{1,0:T(1,128)}) custom-call(bf16[384,768]{1,0:T(8,128)(2,1)} %emb_ref.1, s32[384]{0:T(512)} %label_ref.1, s32[384]{0:T(512)} %index_ref.1), custom_call_target="tpu_custom_call" | custom-call | tf_op jit(solution)/shard_map/build_slots/pallas_call | solution.py:136
  4.6 70.9 %all_to_all.10.got_ref = bf16[512,7,2,128]{3,2,1,0:T(2,128)(2,1)} all-to-all(bf16[512,7,2,128]{3,2,1,0:T(2,128)(2,1)} %get-tuple-element.7), channel_id=1, replica_groups=mesh['owner'=128,'helper'=4] {'owner','helper'}, dimensions={0} | all-to-all | bytes 3670016 | tf_op jit(solution)/shard_map/all_to_all | solution.py:149
  75.6 7.4 %nearest_earlier.1 = f32[512,128]{1,0:T(8,128)} custom-call(bf16[512,7,2,128]{3,2,1,0:T(2,128)(2,1)} %all_to_all.10.got_ref), custom_call_target="tpu_custom_call" | custom-call | tf_op jit(solution)/shard_map/nearest_earlier/pallas_call | solution.py:150
  83.0 26.8 %all_to_all.11 = f32[512,1,128]{2,1,0:T(1,128)} all-to-all(f32[512,1,128]{2,1,0:T(1,128)} %bitcast.5), channel_id=1, replica_groups=mesh['owner'=128,'helper'=4] {'owner','helper'}, dimensions={0} | all-to-all | bytes 524288 | tf_op jit(solution)/shard_map/all_to_all | solution.py:162
  109.8 1.8 %pick.1 = f32[384]{0:T(512)} custom-call(f32[512,128]{1,0:T(8,128)} %bitcast.4, s32[1,384]{1,0:T(1,128)} %get-tuple-element.8.place_ref), custom_call_target="tpu_custom_call" | custom-call | tf_op jit(solution)/shard_map/pick/pallas_call | solution.py:165

commit v3 on v2

v3 whole, which is shorter than its diff:
```python
import functools

import jax
import jax.numpy as jnp
from jax import lax
from jax.experimental import pallas as pl
from jax.experimental.pallas import tpu as pltpu
from jax.sharding import PartitionSpec as P

CLU_DEV = 64
CAP = 2
LANES = 128
BASE = 64
AXES = ("owner", "helper")


def build_slots(
    emb_hbm, label_hbm, index_hbm, slots_ref, place_ref, emb_ref, label_ref, index_ref, sems
):
    rows, features = emb_ref.shape
    count = slots_ref.shape[0]
    copies = [
        pltpu.make_async_copy(label_hbm, label_ref, sems.at[0]),
        pltpu.make_async_copy(index_hbm, index_ref, sems.at[1]),
        pltpu.make_async_copy(emb_hbm, emb_ref, sems.at[2]),
    ]
    for copy in copies:
        copy.start()
    copies[0].wait()
    copies[1].wait()
    label = label_ref[...].reshape(1, rows)
    order = index_ref[...].reshape(1, rows)
    group = label // CLU_DEV
    zero = jnp.zeros_like(label)
    table = jnp.concatenate(
        [
            label - group * CLU_DEV + 1,
            order % BASE,
            (order // BASE) % BASE,
            order // (BASE * BASE),
            group,
            zero,
            zero,
            zero,
        ],
        axis=0,
    ).astype(jnp.float32)
    columns = table.T
    group_column = columns[:, 4:5]
    group_row = group.astype(jnp.float32)
    earlier = lax.broadcasted_iota(jnp.int32, (rows, rows), 0) < lax.broadcasted_iota(
        jnp.int32, (rows, rows), 1
    )
    rank = jnp.sum(
        jnp.where((group_column == group_row) & earlier, 1.0, 0.0), axis=0, keepdims=True
    )
    place = group * CAP + rank.astype(jnp.int32)
    place_ref[...] = place

    total = count * CAP
    chosen = jnp.where(
        lax.broadcasted_iota(jnp.int32, (total, rows), 0) == place, 1.0, 0.0
    ).astype(jnp.bfloat16)
    meta = jnp.concatenate(
        [columns, jnp.zeros((rows, LANES - columns.shape[1]), jnp.float32)], axis=1
    ).astype(jnp.bfloat16)
    copies[2].wait()
    values = emb_ref[...].astype(jnp.float32)
    scale = lax.rsqrt(jnp.sum(values * values, axis=1, keepdims=True) / features + 1e-06)
    unit = (values * scale).astype(jnp.bfloat16)
    for block in range(features // LANES + 1):
        begin = block * LANES
        part = meta if begin == features else unit[:, begin : begin + LANES]
        made = jnp.dot(chosen, part, preferred_element_type=jnp.float32).astype(jnp.bfloat16)
        slots_ref[:, block] = made.reshape(count, CAP, LANES)


def digit_weights(shape, axis, span):
    digit = lax.broadcasted_iota(jnp.int32, shape, axis)
    start = jnp.where(digit == 0, float(span), 0.0)
    within = jnp.where(digit == 1, 1.0, jnp.where(digit == 2, float(BASE), 0.0))
    key = start + jnp.where(digit == 3, float(BASE * BASE), within)
    return start.astype(jnp.bfloat16), key.astype(jnp.bfloat16)


def nearest_earlier(span, got_ref, out_ref, rows_ref, wide_ref):
    count, blocks = got_ref.shape[:2]
    total = count * CAP
    features = (blocks - 1) * LANES
    meta = got_ref[:, blocks - 1].reshape(total, LANES)
    start_weights, key_weights = digit_weights((LANES, LANES), 0, span)
    start_column = jnp.dot(meta, start_weights, preferred_element_type=jnp.float32)
    key_column = jnp.dot(meta, key_weights, preferred_element_type=jnp.float32)
    key_row = lax.dot_general(
        digit_weights((8, LANES), 1, span)[1],
        meta,
        (((1,), (1,)), ((), ())),
        preferred_element_type=jnp.float32,
    )[:1, :]
    for block in range(blocks - 1):
        rows_ref[:, block * LANES : (block + 1) * LANES] = got_ref[:, block].reshape(total, LANES)
    step = 256
    for begin in range(0, total, step):
        part = slice(begin, begin + step)
        scores = lax.dot_general(
            rows_ref[part, :],
            rows_ref[...],
            (((1,), (1,)), ((), ())),
            preferred_element_type=jnp.float32,
        )
        best = jnp.full((step, LANES), -3.0 * features, jnp.float32)
        for column in range(0, total, LANES):
            here = key_row[:, column : column + LANES]
            keep = (here >= start_column[part]) & (here < key_column[part])
            best = jnp.where(keep, jnp.maximum(best, scores[:, column : column + LANES]), best)
        best = jnp.max(best, axis=1, keepdims=True)
        best = jnp.maximum(best / features, -1.0)
        wide_ref[part, :] = jnp.broadcast_to(best, (step, LANES))
    first = wide_ref[pl.ds(0, count, stride=CAP), :]
    second = wide_ref[pl.ds(1, count, stride=CAP), :]
    lane = lax.broadcasted_iota(jnp.int32, first.shape, 1)
    out_ref[...] = jnp.where(lane == 0, first, second)


def pick(returned_ref, place_ref, out_ref):
    count = returned_ref.shape[0]
    rows = place_ref.shape[1]
    place = place_ref[...]
    group = place // CAP
    second = (place - group * CAP) > 0
    value = jnp.where(second, returned_ref[:, 1:2], returned_ref[:, 0:1])
    mine = lax.broadcasted_iota(jnp.int32, (count, rows), 0) == group
    out_ref[...] = jnp.sum(jnp.where(mine, value, 0.0), axis=0)


def on_device(embeddings, labels, row_index):
    rows, features = embeddings.shape
    devices = lax.axis_size("owner") * lax.axis_size("helper")
    total = devices * CAP
    blocks = features // LANES + 1
    params = pltpu.CompilerParams(vmem_limit_bytes=24 * 2**20)
    hbm = pl.BlockSpec(memory_space=pltpu.HBM)
    slots, place = pl.pallas_call(
        build_slots,
        out_shape=(
            jax.ShapeDtypeStruct((devices, blocks, CAP, LANES), jnp.bfloat16),
            jax.ShapeDtypeStruct((1, rows), jnp.int32),
        ),
        in_specs=[hbm, hbm, hbm],
        scratch_shapes=[
            pltpu.VMEM((rows, features), jnp.bfloat16),
            pltpu.VMEM((rows,), jnp.int32),
            pltpu.VMEM((rows,), jnp.int32),
            pltpu.SemaphoreType.DMA((3,)),
        ],
        compiler_params=params,
        name="build_slots",
    )(*(pltpu.with_memory_space_constraint(x, pltpu.HBM) for x in (embeddings, labels, row_index)))
    got = lax.all_to_all(slots, AXES, split_axis=0, concat_axis=0, tiled=True)
    nearest = pl.pallas_call(
        functools.partial(nearest_earlier, rows * devices),
        out_shape=jax.ShapeDtypeStruct((devices, LANES), jnp.float32),
        scratch_shapes=[
            pltpu.VMEM((total, features), jnp.bfloat16),
            pltpu.VMEM((total, LANES), jnp.float32),
        ],
        compiler_params=params,
        name="nearest_earlier",
    )(got)
    returned = lax.all_to_all(
        nearest.reshape(devices, 1, LANES), AXES, split_axis=0, concat_axis=0, tiled=True
    )
    return pl.pallas_call(
        pick,
        out_shape=jax.ShapeDtypeStruct((rows,), jnp.float32),
        compiler_params=params,
        name="pick",
    )(returned.reshape(devices, LANES), place)


def solution(mesh):
    in_specs = (P(AXES, None), P(AXES), P(AXES))
    return jax.shard_map(
        on_device, mesh=mesh, in_specs=in_specs, out_specs=P(AXES), check_vma=False
    )
```

time: 112 us -> 104 us (0.929)
  Pallas kernels: 13.9 us -> 7.17 us
    pallas_call x1, Pallas kernels: 7.44 us -> 3.13 us  [on_device(): pl.pallas_call(functools.partial(nearest_earlier, rows * devices), out_sh...]
    pallas_call x1, Pallas kernels: 4.63 us -> 3.2 us  [on_device(): pl.pallas_call(build_slots, out_shape=(jax.ShapeDtypeStruct((devices, blo...]
where the time goes in v3:
time: 104 us
  blocking collectives  96.7 us (93%)
  Pallas kernels  7.17 us (7%)
    all_to_all x1, blocking collectives, on_device(): got = lax.all_to_all(slots, AXES, split_axis=0, concat_axis=0, tiled=True)  70.6 us
    all_to_all x1, blocking collectives, on_device(): lax.all_to_all(nearest.reshape(devices, 1, LANES), AXES, split_axis=0, co...  26.1 us
    pallas_call x1, Pallas kernels, on_device(): pl.pallas_call(build_slots, out_shape=(jax.ShapeDtypeStruct((devices, blo...  3.2 us
    pallas_call x1, Pallas kernels, on_device(): pl.pallas_call(functools.partial(nearest_earlier, rows * devices), out_sh...  3.13 us

profile of v3, /device:TPU:1, one launch (start us, length us, event | category | flops | bytes accessed | tf_op | source)
XLA Modules:
  0.0 103.9 jit_solution(9759372348570636544)
XLA Ops:
  0.0 3.2 %build_slots.1 = (bf16[512,7,2,128]{3,2,1,0:T(2,128)(2,1)S(1)}, s32[1,384]{1,0:T(1,128)S(1)}) custom-call(bf16[384,768]{1,0:T(8,128)(2,1)} %emb_hbm.1, s32[384]{0:T(512)} %label_hbm.1, s32[384]{0:T(512)} %index_hbm.1), custom_call_target="tpu_custom_call" | custom-call | tf_op jit(solution)/shard_map/build_slots/pallas_call | solution.py:143
  3.2 70.6 %all_to_all.10.got_ref = bf16[512,7,2,128]{3,2,1,0:T(2,128)(2,1)S(1)} all-to-all(bf16[512,7,2,128]{3,2,1,0:T(2,128)(2,1)S(1)} %get-tuple-element.7), channel_id=1, replica_groups=mesh['owner'=128,'helper'=4] {'owner','helper'}, dimensions={0} | all-to-all | bytes 3670016 | tf_op jit(solution)/shard_map/all_to_all | solution.py:159
  73.8 3.1 %nearest_earlier.1 = f32[512,128]{1,0:T(8,128)S(1)} custom-call(bf16[512,7,2,128]{3,2,1,0:T(2,128)(2,1)S(1)} %all_to_all.10.got_ref), custom_call_target="tpu_custom_call" | custom-call | tf_op jit(solution)/shard_map/nearest_earlier/pallas_call | solution.py:160
  77.0 26.1 %all_to_all.11 = f32[512,1,128]{2,1,0:T(1,128)S(1)} all-to-all(f32[512,1,128]{2,1,0:T(1,128)S(1)} %bitcast.5), channel_id=1, replica_groups=mesh['owner'=128,'helper'=4] {'owner','helper'}, dimensions={0} | all-to-all | bytes 524288 | tf_op jit(solution)/shard_map/all_to_all | solution.py:170
  103.0 0.8 pick.1

commit v4 on v3

--- a/solution.py
+++ b/solution.py
@@ -68,11 +68,15 @@
     values = emb_ref[...].astype(jnp.float32)
     scale = lax.rsqrt(jnp.sum(values * values, axis=1, keepdims=True) / features + 1e-06)
     unit = (values * scale).astype(jnp.bfloat16)
-    for block in range(features // LANES + 1):
-        begin = block * LANES
-        part = meta if begin == features else unit[:, begin : begin + LANES]
-        made = jnp.dot(chosen, part, preferred_element_type=jnp.float32).astype(jnp.bfloat16)
-        slots_ref[:, block] = made.reshape(count, CAP, LANES)
+    wide = 2 * LANES
+    for begin in range(0, features + LANES, wide):
+        part = meta if begin == features else unit[:, begin : begin + wide]
+        made = jnp.dot(chosen, part, preferred_element_type=jnp.float32)
+        made = made.astype(jnp.bfloat16)
+        for offset in range(0, part.shape[1], LANES):
+            slots_ref[:, (begin + offset) // LANES] = made[:, offset : offset + LANES].reshape(
+                count, CAP, LANES
+            )
 
 
 def digit_weights(shape, axis, span):
@@ -83,41 +87,69 @@
     return start.astype(jnp.bfloat16), key.astype(jnp.bfloat16)
 
 
-def nearest_earlier(span, got_ref, out_ref, rows_ref, wide_ref):
+def nearest_earlier(span, got_ref, out_ref, rows_ref, best_ref):
     count, blocks = got_ref.shape[:2]
     total = count * CAP
     features = (blocks - 1) * LANES
+    step = 512
+    none = -3.0 * features
     meta = got_ref[:, blocks - 1].reshape(total, LANES)
-    start_weights, key_weights = digit_weights((LANES, LANES), 0, span)
-    start_column = jnp.dot(meta, start_weights, preferred_element_type=jnp.float32)
-    key_column = jnp.dot(meta, key_weights, preferred_element_type=jnp.float32)
-    key_row = lax.dot_general(
-        digit_weights((8, LANES), 1, span)[1],
-        meta,
-        (((1,), (1,)), ((), ())),
-        preferred_element_type=jnp.float32,
-    )[:1, :]
-    for block in range(blocks - 1):
-        rows_ref[:, block * LANES : (block + 1) * LANES] = got_ref[:, block].reshape(total, LANES)
-    step = 256
+    column_weights = digit_weights((LANES, LANES), 0, span)
+    row_weights = digit_weights((8, LANES), 1, span)
+    start_column, key_column = (
+        jnp.dot(meta, weights, preferred_element_type=jnp.float32) for weights in column_weights
+    )
+    start_row, key_row = (
+        lax.dot_general(
+            weights, meta, (((1,), (1,)), ((), ())), preferred_element_type=jnp.float32
+        )[:1, :]
+        for weights in row_weights
+    )
+    crossed = []
+    for begin in range(0, total, step):
+        here = slice(begin, begin + step)
+        for block in range(blocks - 1):
+            rows_ref[here, block * LANES : (block + 1) * LANES] = got_ref[
+                begin // CAP : (begin + step) // CAP, block
+            ].reshape(step, LANES)
+        column_best = jnp.full((8, step), none, jnp.float32)
+        for other in range(0, begin + step, step):
+            part = slice(other, other + step)
+            scores = lax.dot_general(
+                rows_ref[part, :],
+                rows_ref[here, :],
+                (((1,), (1,)), ((), ())),
+                preferred_element_type=jnp.float32,
+            )
+            if other < begin:
+                best = best_ref[part, :]
+            else:
+                best = jnp.full((step, LANES), none, jnp.float32)
+            for lane in range(0, step, LANES):
+                keys = key_row[:, begin + lane : begin + lane + LANES]
+                keep = (keys >= start_column[part]) & (keys < key_column[part])
+                best = jnp.where(keep, jnp.maximum(best, scores[:, lane : lane + LANES]), best)
+            best_ref[part, :] = best
+            if other < begin:
+                keys = jnp.concatenate([key_column[part]] * (step // LANES), axis=1)
+                keep = (keys >= start_row[:, here]) & (keys < key_row[:, here])
+                kept = jnp.where(keep, scores, none)
+                column_best = jnp.maximum(
+                    column_best, jnp.max(kept.reshape(step // 8, 8, step), axis=0)
+                )
+        crossed.append(column_best)
     for begin in range(0, total, step):
         part = slice(begin, begin + step)
-        scores = lax.dot_general(
-            rows_ref[part, :],
-            rows_ref[...],
-            (((1,), (1,)), ((), ())),
-            preferred_element_type=jnp.float32,
-        )
-        best = jnp.full((step, LANES), -3.0 * features, jnp.float32)
-        for column in range(0, total, LANES):
-            here = key_row[:, column : column + LANES]
-            keep = (here >= start_column[part]) & (here < key_column[part])
-            best = jnp.where(keep, jnp.maximum(best, scores[:, column : column + LANES]), best)
+        best = best_ref[part, :]
+        if begin:
+            best = jnp.maximum(
+                best, jnp.concatenate([crossed[begin // step]] * (LANES // 8), axis=0).T
+            )
         best = jnp.max(best, axis=1, keepdims=True)
         best = jnp.maximum(best / features, -1.0)
-        wide_ref[part, :] = jnp.broadcast_to(best, (step, LANES))
-    first = wide_ref[pl.ds(0, count, stride=CAP), :]
-    second = wide_ref[pl.ds(1, count, stride=CAP), :]
+        best_ref[part, :] = jnp.broadcast_to(best, (step, LANES))
+    first = best_ref[pl.ds(0, count, stride=CAP), :]
+    second = best_ref[pl.ds(1, count, stride=CAP), :]
     lane = lax.broadcasted_iota(jnp.int32, first.shape, 1)
     out_ref[...] = jnp.where(lane == 0, first, second)
 

time: 104 us -> 103 us (level)
  no operation moved by 1% of the time
where the time goes in v4:
time: 103 us
  blocking collectives  96.7 us (94%)
  Pallas kernels  6.54 us (6%)
    all_to_all x1, blocking collectives, on_device(): got = lax.all_to_all(slots, AXES, split_axis=0, concat_axis=0, tiled=True)  70.6 us
    all_to_all x1, blocking collectives, on_device(): lax.all_to_all(nearest.reshape(devices, 1, LANES), AXES, split_axis=0, co...  26.1 us
    pallas_call x1, Pallas kernels, on_device(): pl.pallas_call(build_slots, out_shape=(jax.ShapeDtypeStruct((devices, blo...  3.06 us
    pallas_call x1, Pallas kernels, on_device(): pl.pallas_call(functools.partial(nearest_earlier, rows * devices), out_sh...  2.64 us

profile of v4, /device:TPU:1, one launch (start us, length us, event | category | flops | bytes accessed | tf_op | source)
XLA Modules:
  0.0 103.2 jit_solution(5563748008037711219)
XLA Ops:
  0.0 3.1 %build_slots.1 = (bf16[512,7,2,128]{3,2,1,0:T(2,128)(2,1)S(1)}, s32[1,384]{1,0:T(1,128)S(1)}) custom-call(bf16[384,768]{1,0:T(8,128)(2,1)} %emb_hbm.1, s32[384]{0:T(512)} %label_hbm.1, s32[384]{0:T(512)} %index_hbm.1), custom_call_target="tpu_custom_call" | custom-call | tf_op jit(solution)/shard_map/build_slots/pallas_call | solution.py:175
  3.1 70.6 %all_to_all.10.got_ref = bf16[512,7,2,128]{3,2,1,0:T(2,128)(2,1)S(1)} all-to-all(bf16[512,7,2,128]{3,2,1,0:T(2,128)(2,1)S(1)} %get-tuple-element.7), channel_id=1, replica_groups=mesh['owner'=128,'helper'=4] {'owner','helper'}, dimensions={0} | all-to-all | bytes 3670016 | tf_op jit(solution)/shard_map/all_to_all | solution.py:191
  73.7 2.6 %nearest_earlier.1 = f32[512,128]{1,0:T(8,128)S(1)} custom-call(bf16[512,7,2,128]{3,2,1,0:T(2,128)(2,1)S(1)} %all_to_all.10.got_ref), custom_call_target="tpu_custom_call" | custom-call | tf_op jit(solution)/shard_map/nearest_earlier/pallas_call | solution.py:192
  76.3 26.1 %all_to_all.11 = f32[512,1,128]{2,1,0:T(1,128)S(1)} all-to-all(f32[512,1,128]{2,1,0:T(1,128)S(1)} %bitcast.5), channel_id=1, replica_groups=mesh['owner'=128,'helper'=4] {'owner','helper'}, dimensions={0} | all-to-all | bytes 524288 | tf_op jit(solution)/shard_map/all_to_all | solution.py:202
  102.4 0.8 pick.1

commit v5 on v4

--- a/solution.py
+++ b/solution.py
@@ -11,11 +11,13 @@
 CAP = 2
 LANES = 128
 BASE = 64
-AXES = ("owner", "helper")
+CORES = 2
+PEERS = ("ring", "helper")
+ALL = ("ring", "helper", "core")
 
 
 def build_slots(
-    emb_hbm, label_hbm, index_hbm, slots_ref, place_ref, emb_ref, label_ref, index_ref, sems
+    helpers, emb_hbm, label_hbm, index_hbm, slots_ref, place_ref, emb_ref, label_ref, index_ref, sems
 ):
     rows, features = emb_ref.shape
     count = slots_ref.shape[0]
@@ -54,7 +56,9 @@
     rank = jnp.sum(
         jnp.where((group_column == group_row) & earlier, 1.0, 0.0), axis=0, keepdims=True
     )
-    place = group * CAP + rank.astype(jnp.int32)
+    owner = group // helpers
+    chip = (owner // CORES) * helpers + group % helpers
+    place = (chip * CORES + owner % CORES) * CAP + rank.astype(jnp.int32)
     place_ref[...] = place
 
     total = count * CAP
@@ -148,32 +152,45 @@
         best = jnp.max(best, axis=1, keepdims=True)
         best = jnp.maximum(best / features, -1.0)
         best_ref[part, :] = jnp.broadcast_to(best, (step, LANES))
-    first = best_ref[pl.ds(0, count, stride=CAP), :]
-    second = best_ref[pl.ds(1, count, stride=CAP), :]
-    lane = lax.broadcasted_iota(jnp.int32, first.shape, 1)
-    out_ref[...] = jnp.where(lane == 0, first, second)
-
-
-def pick(returned_ref, place_ref, out_ref):
-    count = returned_ref.shape[0]
+    chips = out_ref.shape[0]
+    width = CORES * CAP
+    lane = lax.broadcasted_iota(jnp.int32, out_ref.shape, 1)
+    result = best_ref[pl.ds(0, chips, stride=width), :]
+    for k in range(1, width):
+        result = jnp.where(lane == k, best_ref[pl.ds(k, chips, stride=width), :], result)
+    out_ref[...] = result
+
+
+def pick(core_ref, same_ref, cross_ref, place_ref, out_ref):
+    chips = same_ref.shape[0]
     rows = place_ref.shape[1]
+    core = core_ref[0]
     place = place_ref[...]
-    group = place // CAP
-    second = (place - group * CAP) > 0
-    value = jnp.where(second, returned_ref[:, 1:2], returned_ref[:, 0:1])
-    mine = lax.broadcasted_iota(jnp.int32, (count, rows), 0) == group
+    chip = place // (CORES * CAP)
+    slot = place % CAP
+    same = (place // CAP) % CORES == core
+    mine = lax.broadcasted_iota(jnp.int32, (chips, rows), 0) == chip
+
+    def column(ref, k):
+        return jnp.where(core == 0, ref[:, k : k + 1], ref[:, CAP + k : CAP + k + 1])
+
+    first = jnp.where(same, column(same_ref, 0), column(cross_ref, 0))
+    second = jnp.where(same, column(same_ref, 1), column(cross_ref, 1))
+    value = jnp.where(slot == 0, first, second)
     out_ref[...] = jnp.sum(jnp.where(mine, value, 0.0), axis=0)
 
 
 def on_device(embeddings, labels, row_index):
     rows, features = embeddings.shape
-    devices = lax.axis_size("owner") * lax.axis_size("helper")
+    helpers = lax.axis_size("helper")
+    chips = lax.axis_size("ring") * helpers
+    devices = chips * CORES
     total = devices * CAP
     blocks = features // LANES + 1
     params = pltpu.CompilerParams(vmem_limit_bytes=24 * 2**20)
     hbm = pl.BlockSpec(memory_space=pltpu.HBM)
     slots, place = pl.pallas_call(
-        build_slots,
+        functools.partial(build_slots, helpers),
         out_shape=(
             jax.ShapeDtypeStruct((devices, blocks, CAP, LANES), jnp.bfloat16),
             jax.ShapeDtypeStruct((1, rows), jnp.int32),
@@ -188,10 +205,10 @@
         compiler_params=params,
         name="build_slots",
     )(*(pltpu.with_memory_space_constraint(x, pltpu.HBM) for x in (embeddings, labels, row_index)))
-    got = lax.all_to_all(slots, AXES, split_axis=0, concat_axis=0, tiled=True)
+    got = lax.all_to_all(slots, ALL, split_axis=0, concat_axis=0, tiled=True)
     nearest = pl.pallas_call(
         functools.partial(nearest_earlier, rows * devices),
-        out_shape=jax.ShapeDtypeStruct((devices, LANES), jnp.float32),
+        out_shape=jax.ShapeDtypeStruct((chips, LANES), jnp.float32),
         scratch_shapes=[
             pltpu.VMEM((total, features), jnp.bfloat16),
             pltpu.VMEM((total, LANES), jnp.float32),
@@ -200,18 +217,29 @@
         name="nearest_earlier",
     )(got)
     returned = lax.all_to_all(
-        nearest.reshape(devices, 1, LANES), AXES, split_axis=0, concat_axis=0, tiled=True
-    )
+        nearest.reshape(chips, 1, LANES), PEERS, split_axis=0, concat_axis=0, tiled=True
+    ).reshape(chips, LANES)
+    crossed = lax.ppermute(returned, "core", [(k, CORES - 1 - k) for k in range(CORES)])
+    vmem = pl.BlockSpec(memory_space=pltpu.VMEM)
     return pl.pallas_call(
         pick,
         out_shape=jax.ShapeDtypeStruct((rows,), jnp.float32),
+        in_specs=[pl.BlockSpec(memory_space=pltpu.SMEM), vmem, vmem, vmem],
         compiler_params=params,
         name="pick",
-    )(returned.reshape(devices, LANES), place)
+    )(lax.axis_index("core").astype(jnp.int32).reshape(1), returned, crossed, place)
 
 
 def solution(mesh):
-    in_specs = (P(AXES, None), P(AXES), P(AXES))
+    owners, helpers = mesh.devices.shape
+    chips = jax.sharding.Mesh(
+        mesh.devices.reshape(owners // CORES, CORES, helpers), ("ring", "core", "helper")
+    )
+    split = ("ring", "core", "helper")
     return jax.shard_map(
-        on_device, mesh=mesh, in_specs=in_specs, out_specs=P(AXES), check_vma=False
-    )
+        on_device,
+        mesh=chips,
+        in_specs=(P(split, None), P(split), P(split)),
+        out_specs=P(split),
+        check_vma=False,
+    )

time: 103 us -> 105 us (1.019)
  starting transfers between devices: 0 us -> 3.9 us
  blocking collectives: 96.7 us -> 93.3 us
    ppermute x0 -> x1, starting transfers between devices: none -> 3.9 us  [on_device(): lax.ppermute(returned, 'core', [(k, CORES - 1 - k) for k in range(CORES)])]
    all_to_all x2, blocking collectives: 96.7 us -> 93.3 us  [the longest x1 70.3 us: on_device(): got = lax.all_to_all(slots, ALL, split_axis=0, concat_axis=0, tiled=True)]
  transfers between devices with their start and end apart: 0 -> 1, of which waited for: 0 -> 1; matrix products, arithmetic and copies ran while one was open for 0% -> 0% of each run, Pallas kernels for 0% -> 0%
where the time goes in v5:
time: 105 us
  blocking collectives  93.3 us (89%)
  Pallas kernels  6.55 us (6%)
  starting transfers between devices  3.9 us (4%)
    all_to_all x1, blocking collectives, on_device(): got = lax.all_to_all(slots, ALL, split_axis=0, concat_axis=0, tiled=True)  70.3 us
    all_to_all x1, blocking collectives, on_device(): lax.all_to_all(nearest.reshape(chips, 1, LANES), PEERS, split_axis=0, con...  23 us
    ppermute x1, starting transfers between devices, on_device(): lax.ppermute(returned, 'core', [(k, CORES - 1 - k) for k in range(CORES)])  3.9 us
    pallas_call x1, Pallas kernels, on_device(): pl.pallas_call(functools.partial(build_slots, helpers), out_shape=(jax.Sh...  3.05 us
    pallas_call x1, Pallas kernels, on_device(): pl.pallas_call(functools.partial(nearest_earlier, rows * devices), out_sh...  2.6 us
  transfers between devices with their start and end apart: 1, of which 1 were waited for; matrix products, arithmetic and copies ran while one was open for 0% of the time, Pallas kernels for 0%

profile of v5, /device:TPU:1, one launch (start us, length us, event | category | flops | bytes accessed | tf_op | source)
XLA Modules:
  0.0 104.7 jit_solution(17649178172544270937)
XLA Ops:
  0.0 3.0 %build_slots.1 = (bf16[512,7,2,128]{3,2,1,0:T(2,128)(2,1)S(1)}, s32[1,384]{1,0:T(1,128)S(1)}) custom-call(bf16[384,768]{1,0:T(8,128)(2,1)} %emb_hbm.1, s32[384]{0:T(512)} %label_hbm.1, s32[384]{0:T(512)} %index_hbm.1), custom_call_target="tpu_custom_call" | custom-call | tf_op jit(solution)/shard_map/build_slots/pallas_call | solution.py:192
  3.1 70.3 %all_to_all.10.got_ref = bf16[512,7,2,128]{3,2,1,0:T(2,128)(2,1)S(1)} all-to-all(bf16[512,7,2,128]{3,2,1,0:T(2,128)(2,1)S(1)} %get-tuple-element.7), channel_id=1, replica_groups=mesh['ring'=64,'core'=2,'helper'=4] {'ring','helper','core'}, dimensions={0} | all-to-all | bytes 3670016 | tf_op jit(solution)/shard_map/all_to_all | solution.py:208
  73.3 2.6 %nearest_earlier.1 = f32[256,128]{1,0:T(8,128)S(1)} custom-call(bf16[512,7,2,128]{3,2,1,0:T(2,128)(2,1)S(1)} %all_to_all.10.got_ref), custom_call_target="tpu_custom_call" | custom-call | tf_op jit(solution)/shard_map/nearest_earlier/pallas_call | solution.py:209
  75.9 23.0 %all_to_all.11 = f32[256,1,128]{2,1,0:T(1,128)S(1)} all-to-all(f32[256,1,128]{2,1,0:T(1,128)S(1)} %bitcast.7), channel_id=1, replica_groups=mesh['ring'=64,'core'=2,'helper'=4] {'ring','helper'}, dimensions={0} | all-to-all | bytes 262144 | tf_op jit(solution)/shard_map/all_to_all | solution.py:219
  99.0 3.9 %collective-permute-start = (f32[256,128]{1,0:T(8,128)S(1)}, f32[256,128]{1,0:T(8,128)S(1)}, u32[]{:S(2)}, u32[]{:S(2)}) collective-permute-start(f32[256,128]{1,0:T(8,128)S(1)} %bitcast.5), channel_id=1, source_target_pairs={{0,4},{4,0},{1,5},{5,1},{2,6},{6,2},{3,7},{7,3},{8,12},{12,8},{9,1... | collective-permute-start | bytes 393224 | tf_op jit(solution)/shard_map/ppermute | solution.py:222
  102.9 1.0 collective-permute-done.cross_ref
  103.8 0.9 pick.1
Async XLA Ops:
  99.0 4.9 %collective-permute-start = (f32[256,128]{1,0:T(8,128)S(1)}, f32[256,128]{1,0:T(8,128)S(1)}, u32[]{:S(2)}, u32[]{:S(2)}) collective-permute-start(f32[256,128]{1,0:T(8,128)S(1)} %bitcast.5), channel_id=1, source_target_pairs={{0,4},{4,0},{1,5},{5,1},{2,6},{6,2},{3,7},{7,3},{8,12},{12,8},{9,1... | collective-permute-start | bytes 393224 | tf_op jit(solution)/shard_map/ppermute | solution.py:222

commit v6 on v5

--- a/solution.py
+++ b/solution.py
@@ -12,12 +12,12 @@
 LANES = 128
 BASE = 64
 CORES = 2
-PEERS = ("ring", "helper")
-ALL = ("ring", "helper", "core")
+PEERS = ("helper", "ring")
+ALL = ("ring", "core", "helper")
 
 
 def build_slots(
-    helpers, emb_hbm, label_hbm, index_hbm, slots_ref, place_ref, emb_ref, label_ref, index_ref, sems
+    emb_hbm, label_hbm, index_hbm, slots_ref, place_ref, emb_ref, label_ref, index_ref, sems
 ):
     rows, features = emb_ref.shape
     count = slots_ref.shape[0]
@@ -56,9 +56,7 @@
     rank = jnp.sum(
         jnp.where((group_column == group_row) & earlier, 1.0, 0.0), axis=0, keepdims=True
     )
-    owner = group // helpers
-    chip = (owner // CORES) * helpers + group % helpers
-    place = (chip * CORES + owner % CORES) * CAP + rank.astype(jnp.int32)
+    place = group * CAP + rank.astype(jnp.int32)
     place_ref[...] = place
 
     total = count * CAP
@@ -91,7 +89,7 @@
     return start.astype(jnp.bfloat16), key.astype(jnp.bfloat16)
 
 
-def nearest_earlier(span, got_ref, out_ref, rows_ref, best_ref):
+def nearest_earlier(span, helpers, got_ref, out_ref, rows_ref, best_ref):
     count, blocks = got_ref.shape[:2]
     total = count * CAP
     features = (blocks - 1) * LANES
@@ -152,23 +150,28 @@
         best = jnp.max(best, axis=1, keepdims=True)
         best = jnp.maximum(best / features, -1.0)
         best_ref[part, :] = jnp.broadcast_to(best, (step, LANES))
-    chips = out_ref.shape[0]
-    width = CORES * CAP
-    lane = lax.broadcasted_iota(jnp.int32, out_ref.shape, 1)
-    result = best_ref[pl.ds(0, chips, stride=width), :]
-    for k in range(1, width):
-        result = jnp.where(lane == k, best_ref[pl.ds(k, chips, stride=width), :], result)
-    out_ref[...] = result
-
-
-def pick(core_ref, same_ref, cross_ref, place_ref, out_ref):
+    rings = out_ref.shape[0] // helpers
+    near = helpers * CAP
+    lane = lax.broadcasted_iota(jnp.int32, (rings, LANES), 1)
+    for helper in range(helpers):
+        result = jnp.zeros((rings, LANES), jnp.float32)
+        for k in range(CORES * CAP):
+            start = (k // CAP) * near + helper * CAP + k % CAP
+            value = best_ref[pl.ds(start, rings, stride=CORES * near), :]
+            result = jnp.where(lane == k, value, result)
+        out_ref[helper * rings : (helper + 1) * rings, :] = result
+
+
+def pick(helpers, core_ref, same_ref, cross_ref, place_ref, out_ref):
     chips = same_ref.shape[0]
     rows = place_ref.shape[1]
     core = core_ref[0]
     place = place_ref[...]
-    chip = place // (CORES * CAP)
+    group = place // CAP
+    owner = group // helpers
+    chip = (group - owner * helpers) * (chips // helpers) + owner // CORES
     slot = place % CAP
-    same = (place // CAP) % CORES == core
+    same = owner % CORES == core
     mine = lax.broadcasted_iota(jnp.int32, (chips, rows), 0) == chip
 
     def column(ref, k):
@@ -190,7 +193,7 @@
     params = pltpu.CompilerParams(vmem_limit_bytes=24 * 2**20)
     hbm = pl.BlockSpec(memory_space=pltpu.HBM)
     slots, place = pl.pallas_call(
-        functools.partial(build_slots, helpers),
+        build_slots,
         out_shape=(
             jax.ShapeDtypeStruct((devices, blocks, CAP, LANES), jnp.bfloat16),
             jax.ShapeDtypeStruct((1, rows), jnp.int32),
@@ -207,7 +210,7 @@
     )(*(pltpu.with_memory_space_constraint(x, pltpu.HBM) for x in (embeddings, labels, row_index)))
     got = lax.all_to_all(slots, ALL, split_axis=0, concat_axis=0, tiled=True)
     nearest = pl.pallas_call(
-        functools.partial(nearest_earlier, rows * devices),
+        functools.partial(nearest_earlier, rows * devices, helpers),
         out_shape=jax.ShapeDtypeStruct((chips, LANES), jnp.float32),
         scratch_shapes=[
             pltpu.VMEM((total, features), jnp.bfloat16),
@@ -222,7 +225,7 @@
     crossed = lax.ppermute(returned, "core", [(k, CORES - 1 - k) for k in range(CORES)])
     vmem = pl.BlockSpec(memory_space=pltpu.VMEM)
     return pl.pallas_call(
-        pick,
+        functools.partial(pick, helpers),
         out_shape=jax.ShapeDtypeStruct((rows,), jnp.float32),
         in_specs=[pl.BlockSpec(memory_space=pltpu.SMEM), vmem, vmem, vmem],
         compiler_params=params,

time: 105 us -> 105 us (level)
  no operation moved by 1% of the time
where the time goes in v6:
time: 105 us
  blocking collectives  93.2 us (89%)
  Pallas kernels  6.61 us (6%)
  starting transfers between devices  4.1 us (4%)
    all_to_all x1, blocking collectives, on_device(): got = lax.all_to_all(slots, ALL, split_axis=0, concat_axis=0, tiled=True)  70.6 us
    all_to_all x1, blocking collectives, on_device(): lax.all_to_all(nearest.reshape(chips, 1, LANES), PEERS, split_axis=0, con...  22.6 us
    ppermute x1, starting transfers between devices, on_device(): lax.ppermute(returned, 'core', [(k, CORES - 1 - k) for k in range(CORES)])  4.1 us
    pallas_call x1, Pallas kernels, on_device(): pl.pallas_call(build_slots, out_shape=(jax.ShapeDtypeStruct((devices, blo...  3.06 us
    pallas_call x1, Pallas kernels, on_device(): pl.pallas_call(functools.partial(nearest_earlier, rows * devices, helpers...  2.65 us
  transfers between devices with their start and end apart: 1, of which 1 were waited for; matrix products, arithmetic and copies ran while one was open for 0% of the time, Pallas kernels for 0%

profile of v6, /device:TPU:1, one launch (start us, length us, event | category | flops | bytes accessed | tf_op | source)
XLA Modules:
  0.0 104.9 jit_solution(2051685062607356609)
XLA Ops:
  0.0 3.1 %build_slots.1 = (bf16[512,7,2,128]{3,2,1,0:T(2,128)(2,1)S(1)}, s32[1,384]{1,0:T(1,128)S(1)}) custom-call(bf16[384,768]{1,0:T(8,128)(2,1)} %emb_hbm.1, s32[384]{0:T(512)} %label_hbm.1, s32[384]{0:T(512)} %index_hbm.1), custom_call_target="tpu_custom_call" | custom-call | tf_op jit(solution)/shard_map/build_slots/pallas_call | solution.py:195
  3.1 70.6 %all_to_all.10.got_ref = bf16[512,7,2,128]{3,2,1,0:T(2,128)(2,1)S(1)} all-to-all(bf16[512,7,2,128]{3,2,1,0:T(2,128)(2,1)S(1)} %get-tuple-element.7), channel_id=1, replica_groups=mesh['ring'=64,'core'=2,'helper'=4] {'ring','core','helper'}, dimensions={0} | all-to-all | bytes 3670016 | tf_op jit(solution)/shard_map/all_to_all | solution.py:211
  73.7 2.6 %nearest_earlier.1 = f32[256,128]{1,0:T(8,128)S(1)} custom-call(bf16[512,7,2,128]{3,2,1,0:T(2,128)(2,1)S(1)} %all_to_all.10.got_ref), custom_call_target="tpu_custom_call" | custom-call | tf_op jit(solution)/shard_map/nearest_earlier/pallas_call | solution.py:212
  76.3 22.6 %all_to_all.11 = f32[256,1,128]{2,1,0:T(1,128)S(1)} all-to-all(f32[256,1,128]{2,1,0:T(1,128)S(1)} %bitcast.7), channel_id=1, replica_groups=mesh['ring'=64,'core'=2,'helper'=4] {'helper','ring'}, dimensions={0} | all-to-all | bytes 262144 | tf_op jit(solution)/shard_map/all_to_all | solution.py:222
  98.9 4.1 %collective-permute-start = (f32[256,128]{1,0:T(8,128)S(1)}, f32[256,128]{1,0:T(8,128)S(1)}, u32[]{:S(2)}, u32[]{:S(2)}) collective-permute-start(f32[256,128]{1,0:T(8,128)S(1)} %bitcast.5), channel_id=1, source_target_pairs={{0,4},{4,0},{1,5},{5,1},{2,6},{6,2},{3,7},{7,3},{8,12},{12,8},{9,1... | collective-permute-start | bytes 393224 | tf_op jit(solution)/shard_map/ppermute | solution.py:225
  103.1 1.0 collective-permute-done.cross_ref
  104.0 0.9 pick.1
Async XLA Ops:
  98.9 5.1 %collective-permute-start = (f32[256,128]{1,0:T(8,128)S(1)}, f32[256,128]{1,0:T(8,128)S(1)}, u32[]{:S(2)}, u32[]{:S(2)}) collective-permute-start(f32[256,128]{1,0:T(8,128)S(1)} %bitcast.5), channel_id=1, source_target_pairs={{0,4},{4,0},{1,5},{5,1},{2,6},{6,2},{3,7},{7,3},{8,12},{12,8},{9,1... | collective-permute-start | bytes 393224 | tf_op jit(solution)/shard_map/ppermute | solution.py:225

commit v7 on v4

--- a/solution.py
+++ b/solution.py
@@ -19,10 +19,12 @@
 ):
     rows, features = emb_ref.shape
     count = slots_ref.shape[0]
+    half = rows // 2
     copies = [
         pltpu.make_async_copy(label_hbm, label_ref, sems.at[0]),
         pltpu.make_async_copy(index_hbm, index_ref, sems.at[1]),
-        pltpu.make_async_copy(emb_hbm, emb_ref, sems.at[2]),
+        pltpu.make_async_copy(emb_hbm.at[:half], emb_ref.at[:half], sems.at[2]),
+        pltpu.make_async_copy(emb_hbm.at[half:], emb_ref.at[half:], sems.at[3]),
     ]
     for copy in copies:
         copy.start()
@@ -64,10 +66,13 @@
     meta = jnp.concatenate(
         [columns, jnp.zeros((rows, LANES - columns.shape[1]), jnp.float32)], axis=1
     ).astype(jnp.bfloat16)
-    copies[2].wait()
-    values = emb_ref[...].astype(jnp.float32)
-    scale = lax.rsqrt(jnp.sum(values * values, axis=1, keepdims=True) / features + 1e-06)
-    unit = (values * scale).astype(jnp.bfloat16)
+    parts = []
+    for part in range(2):
+        copies[2 + part].wait()
+        values = emb_ref[part * half : (part + 1) * half, :].astype(jnp.float32)
+        mean = jnp.sum(values * values, axis=1, keepdims=True) / features
+        parts.append((values * lax.rsqrt(mean + 1e-06)).astype(jnp.bfloat16))
+    unit = jnp.concatenate(parts, axis=0)
     wide = 2 * LANES
     for begin in range(0, features + LANES, wide):
         part = meta if begin == features else unit[:, begin : begin + wide]
@@ -183,7 +188,7 @@
             pltpu.VMEM((rows, features), jnp.bfloat16),
             pltpu.VMEM((rows,), jnp.int32),
             pltpu.VMEM((rows,), jnp.int32),
-            pltpu.SemaphoreType.DMA((3,)),
+            pltpu.SemaphoreType.DMA((4,)),
         ],
         compiler_params=params,
         name="build_slots",

time: 103 us -> 104 us (level)
  no operation moved by 1% of the time
where the time goes in v7:
time: 104 us; the launch traced here: 103 us
  blocking collectives  96.7 us (93%)
  Pallas kernels  6.65 us (6%)
    all_to_all x1, blocking collectives, on_device(): got = lax.all_to_all(slots, AXES, split_axis=0, concat_axis=0, tiled=True)  70.6 us
    all_to_all x1, blocking collectives, on_device(): lax.all_to_all(nearest.reshape(devices, 1, LANES), AXES, split_axis=0, co...  26.1 us
    pallas_call x1, Pallas kernels, on_device(): pl.pallas_call(build_slots, out_shape=(jax.ShapeDtypeStruct((devices, blo...  3.16 us
    pallas_call x1, Pallas kernels, on_device(): pl.pallas_call(functools.partial(nearest_earlier, rows * devices), out_sh...  2.64 us

profile of v7, /device:TPU:1, one launch (start us, length us, event | category | flops | bytes accessed | tf_op | source)
XLA Modules:
  0.0 103.3 jit_solution(11206996446326948448)
XLA Ops:
  0.0 3.2 %build_slots.1 = (bf16[512,7,2,128]{3,2,1,0:T(2,128)(2,1)S(1)}, s32[1,384]{1,0:T(1,128)S(1)}) custom-call(bf16[384,768]{1,0:T(8,128)(2,1)} %emb_hbm.1, s32[384]{0:T(512)} %label_hbm.1, s32[384]{0:T(512)} %index_hbm.1), custom_call_target="tpu_custom_call" | custom-call | tf_op jit(solution)/shard_map/build_slots/pallas_call | solution.py:180
  3.2 70.6 %all_to_all.10.got_ref = bf16[512,7,2,128]{3,2,1,0:T(2,128)(2,1)S(1)} all-to-all(bf16[512,7,2,128]{3,2,1,0:T(2,128)(2,1)S(1)} %get-tuple-element.7), channel_id=1, replica_groups=mesh['owner'=128,'helper'=4] {'owner','helper'}, dimensions={0} | all-to-all | bytes 3670016 | tf_op jit(solution)/shard_map/all_to_all | solution.py:196
  73.8 2.6 %nearest_earlier.1 = f32[512,128]{1,0:T(8,128)S(1)} custom-call(bf16[512,7,2,128]{3,2,1,0:T(2,128)(2,1)S(1)} %all_to_all.10.got_ref), custom_call_target="tpu_custom_call" | custom-call | tf_op jit(solution)/shard_map/nearest_earlier/pallas_call | solution.py:197
  76.4 26.1 %all_to_all.11 = f32[512,1,128]{2,1,0:T(1,128)S(1)} all-to-all(f32[512,1,128]{2,1,0:T(1,128)S(1)} %bitcast.5), channel_id=1, replica_groups=mesh['owner'=128,'helper'=4] {'owner','helper'}, dimensions={0} | all-to-all | bytes 524288 | tf_op jit(solution)/shard_map/all_to_all | solution.py:207
  102.5 0.8 pick.1
